TPU v7x, 256 devices: a whole 4x4x8 slice. The times are simulated.
256 devices in a mesh: expert: 32 (over x, z), tensor: 8 (over y, core).
Axes of the slice: x: 4, y: 4, z: 8, core: 2. Of those that a mesh axis runs over, the one named last changes fastest.
Arguments:
- tokens: bfloat16 [8192, 4096], P('expert'), may hold values from -6 to 6
- cotangent: bfloat16 [8192, 4096], P('expert'), may hold values from -1.5 to 1.5
- w_in: bfloat16 [4096, 65536], P(None, ('expert', 'tensor')), may hold values from -0.09375 to 0.09375
- w_out: bfloat16 [65536, 4096], P(('expert', 'tensor')), may hold values from -0.09375 to 0.09375
- router: bfloat16 [4096, 16], replicated, may hold values from -0.09375 to 0.09375
- chosen: int32 [16, 512], replicated, may hold values from 0 to 8191, as said below
Outputs:
- grad_tokens: bfloat16 [8192, 4096], P('expert', 'tensor')
- grad_in: bfloat16 [4096, 65536], P(None, ('expert', 'tensor'))
- grad_out: bfloat16 [65536, 4096], P(('expert', 'tensor'))
- grad_router: float32 [4096, 16], replicated
Inputs may be any that keep to these rules, and one draw needn't show every extreme that they name: Row e lists, in increasing order, 512 distinct tokens chosen by expert e; at most 32 of them lie among one device's 256 consecutive tokens, and in every row some device's tokens hold exactly 32 of them.
All inputs are finite; a program needn't handle non-finite values.
Results may differ from a plain program's by a relative error of at most 0.005.
Values may be sent and summed in bfloat16 or wider, within the bound.
A program may use at most 128 MiB of HBM per device.

v0:
```python
import jax
import jax.numpy as jnp
from jax import lax
from jax.sharding import PartitionSpec as P


def body(tokens, cotangent, w_in, w_out, router, chosen):
    tok_dev, features = tokens.shape
    n_expert = lax.axis_size("expert")
    bucket = 4 * tok_dev // n_expert
    capacity = chosen.shape[1]
    expert_total = router.shape[1]
    device_index = lax.axis_index("expert")
    expert = device_index // 2
    slot_range = jnp.arange(bucket, dtype=jnp.int32)
    first_token = device_index * tok_dev
    starts = jnp.sum((chosen < first_token).astype(jnp.int32), axis=1)
    run_ends = jnp.sum((chosen < first_token + tok_dev).astype(jnp.int32), axis=1)
    counts = run_ends - starts
    positions = jnp.minimum(starts[:, None] + slot_range[None, :], capacity - 1)
    picked = jnp.take_along_axis(chosen, positions, axis=1) - first_token
    filled = slot_range[None, :] < counts[:, None]
    local_rows = jnp.where(filled, picked, 0)
    owner_expert = jnp.arange(n_expert, dtype=jnp.int32) // 2
    send_rows = local_rows[owner_expert].reshape(-1)
    send_filled = filled[owner_expert].reshape(-1)

    def pack(source):
        gathered = jnp.where(send_filled[:, None], source[send_rows], jnp.zeros((), source.dtype))
        return gathered.reshape(n_expert, bucket, source.shape[1])

    got_x, got_y = (
        lax.all_to_all(pack(tokens), "expert", split_axis=0, concat_axis=0, tiled=True),
        lax.all_to_all(pack(cotangent), "expert", split_axis=0, concat_axis=0, tiled=True),
    )
    my_chosen = lax.dynamic_index_in_dim(chosen, expert, 0, keepdims=False)
    home_index = my_chosen // tok_dev
    bounds = jnp.arange(n_expert, dtype=jnp.int32) * tok_dev
    run_start = jnp.sum((my_chosen[None, :] < bounds[:, None]).astype(jnp.int32), axis=1)
    slot_index = home_index * bucket + jnp.arange(capacity, dtype=jnp.int32) - run_start[home_index]
    x_rows = got_x.reshape(-1, features)[slot_index]
    grad_rows = got_y.reshape(-1, features)[slot_index]
    r_col = lax.dynamic_slice_in_dim(router, expert, 1, 1)
    gate = jax.nn.sigmoid(jnp.dot(x_rows, r_col, preferred_element_type=jnp.float32)[:, 0])
    pre_act = jnp.dot(x_rows, w_in, preferred_element_type=jnp.float32)
    sig_act = jax.nn.sigmoid(pre_act)
    hidden = pre_act * sig_act
    upstream = jnp.dot(grad_rows, w_out.T, preferred_element_type=jnp.float32)
    gated_hidden = (gate[:, None] * hidden).astype(jnp.bfloat16)
    gate_grad = jnp.sum(hidden * upstream, axis=1)
    pre_grad = (gate[:, None] * upstream * sig_act * (1.0 + pre_act * (1.0 - sig_act))).astype(
        jnp.bfloat16
    )
    grad_out = jnp.dot(gated_hidden.T, grad_rows, preferred_element_type=jnp.float32).astype(
        jnp.bfloat16
    )
    grad_in = jnp.dot(x_rows.T, pre_grad, preferred_element_type=jnp.float32).astype(jnp.bfloat16)
    score_grad = gate_grad * gate * (1.0 - gate)
    router_col = jnp.dot(score_grad, x_rows.astype(jnp.float32), precision=lax.Precision.HIGHEST)
    router_term = (
        router_col[:, None] * (jnp.arange(expert_total) == expert).astype(jnp.float32)[None, :]
    )
    grad_router = lax.psum(router_term, ("expert", "tensor"))
    router_rows = r_col.astype(jnp.float32)
    summed = lax.psum_scatter(
        jnp.dot(w_in, pre_grad.T, preferred_element_type=jnp.float32)
        + router_rows * score_grad[None, :],
        "tensor",
        scatter_dimension=0,
        tiled=True,
    )
    share = summed.shape[0]
    outgoing = jnp.zeros((share, n_expert * bucket), jnp.float32).at[:, slot_index].set(summed)
    returned = lax.all_to_all(
        outgoing.reshape(share, n_expert, bucket), "expert", split_axis=1, concat_axis=1, tiled=True
    )
    returned = jnp.where(send_filled[None, :], returned.reshape(share, -1), 0.0)
    combined = jnp.zeros((share, tok_dev), jnp.float32).at[:, send_rows].add(returned)
    grad_tokens = combined.T.astype(jnp.bfloat16)
    return (grad_tokens, grad_in, grad_out, grad_router)


def solution(mesh):
    placed = (
        P("expert", None),
        P("expert", None),
        P(None, ("expert", "tensor")),
        P(("expert", "tensor"), None),
        P(),
        P(),
    )
    return jax.shard_map(
        body,
        mesh=mesh,
        in_specs=placed,
        out_specs=(
            P("expert", "tensor"),
            P(None, ("expert", "tensor")),
            P(("expert", "tensor"), None),
            P(),
        ),
        check_vma=False,
    )
```

profile of v0, /device:TPU:2, one launch (start us, length us, event | category | flops | bytes accessed | tf_op | source)
XLA Modules:
  0.0 806.7 jit_solution(2339139497223671526)
XLA Ops:
  8.0 0.0 copy-start
  8.0 0.0 copy-start.2
  8.1 1.0 convert_reduce_fusion.2
  9.1 0.1 fusion.13
  9.2 0.1 reshape.418
  9.2 0.0 copy-done.2
  9.2 4.5 gather_fusion.6
  13.8 0.1 reshape.421
  13.8 0.1 iota_compare_fusion
  13.9 0.1 subtract_select_fusion
  14.0 0.6 gather_fusion
  14.6 0.1 reshape.325
  14.7 0.6 gather_fusion.1
  15.3 0.0 copy-done
  15.3 7.8 gather_fusion.4
  23.1 16.9 %gather_fusion.2 = bf16[1024,4096]{1,0:T(8,128)(2,1)} fusion(bf16[256,4096]{1,0:T(8,128)(2,1)} %param.6, s32[1024]{0:T(1024)S(1)} %broadcast_clamp_fusion), kind=kCustom, calls=%fused_computation.2 | custom fusion | bytes 16781312 | tf_op jit(solution)/shard_map/gather | solution.py:29
  40.0 9.2 %broadcast_select_fusion = (bf16[32,32,4096]{2,1,0:T(8,128)(2,1)}, bf16[32,32,4096]{2,1,0:T(8,128)(2,1)S(1)}) fusion(bf16[32,32,4096]{2,1,0:T(8,128)(2,1)} %bitcast.83, pred[32,32]{1,0:T(8,128)(4,1)S(1)} %gather_fusion.1, bf16[32,32,4096]{2,1,0:T(8,128)(2,1)} %bitcast.84), kind=kLoop, calls=%fused_computation.10 | loop fusion | flops 8388608 | bytes 33555456 | tf_op jit(solution)/shard_map/jit(_where)/select_n | solution.py:29
  49.2 194.9 %all_to_all.15 = bf16[32,32,4096]{2,1,0:T(8,128)(2,1)} all-to-all(bf16[32,32,4096]{2,1,0:T(8,128)(2,1)S(1)} %get-tuple-element.37), channel_id=1, replica_groups=mesh['expert'=32,'tensor'=8] {'expert'}, dimensions={0} | all-to-all | bytes 16777216 | tf_op jit(solution)/shard_map/all_to_all | solution.py:33
  244.1 7.7 all-to-all-start.1
  251.8 0.0 reduce-scatter.2.cloned.1.call-start
  251.9 0.9 dynamic-slice_reduce_fusion
  252.8 0.2 convert_reduce_fusion
  253.0 0.7 fusion.21
  253.7 4.3 compare_select_fusion.5
  258.1 0.7 fusion.20
  258.8 0.2 compare_reduce_fusion.24
  258.9 15.5 %select_select_fusion = s32[512]{0:T(512)S(1)} fusion(pred[512]{0:T(512)(128)(4,1)S(1)} %get-tuple-element.30, pred[512]{0:T(512)(128)(4,1)S(1)} %get-tuple-element.29, pred[512]{0:T(512)(128)(4,1)S(1)} %get-tuple-element.28, pred[512]{0:T(512)(128)(4,1)S(1)} %get-tuple-element.27, pred[512]{0:T(512)(128)(4,1)S(1)} %get-tuple-element.26, ...), kind=kLoop, calls=%fused_computation.88 | loop fusion | flops 12800 | bytes 16996 | tf_op jit(solution)/shard_map/gather | solution.py:40
  274.5 0.0 copy-start.5
  274.5 13.3 %gather_fusion.3 = bf16[512,4096]{1,0:T(8,128)(2,1)} fusion(bf16[1024,4096]{1,0:T(8,128)(2,1)} %bitcast.82, s32[1024]{0:T(1024)S(1)} %pad_clamp_fusion), kind=kCustom, calls=%fused_computation.3 | custom fusion | bytes 8390656 | tf_op jit(solution)/shard_map/gather | solution.py:41
  287.9 0.0 copy-start.3
  287.9 3.5 fusion.9
  291.4 0.0 copy-done.5
  291.4 0.0 copy-done.3
  291.4 1.3 fusion.22
  292.7 144.1 %all-to-all-done.1 = bf16[32,32,4096]{2,1,0:T(8,128)(2,1)} async-done(((bf16[32,32,4096]{2,1,0:T(8,128)(2,1)}), bf16[32,32,4096]{2,1,0:T(8,128)(2,1)}, u32[]{:S(2)}, u32[]{:S(2)}) %all-to-all-start.1) | async-done | bytes 8388640 | tf_op jit(solution)/shard_map/all_to_all | solution.py:34
  436.9 13.0 %gather_fusion.5 = bf16[512,4096]{1,0:T(8,128)(2,1)} fusion(bf16[1024,4096]{1,0:T(8,128)(2,1)} %bitcast.43, s32[1024]{0:T(1024)S(1)} %pad_clamp_fusion), kind=kCustom, calls=%fused_computation.5 | custom fusion | bytes 8390656 | tf_op jit(solution)/shard_map/gather | solution.py:42
  449.9 4.3 multiply_reduce_fusion
  454.2 5.1 bitcast_add_fusion
  459.3 0.0 reduce-scatter.2.cloned.1.call-update
  459.3 57.6 %reduce-scatter.2.cloned.1.call-done = f32[512,512]{0,1:T(8,128)} async-done(((f32[4096,512]{0,1:T(8,128)}), f32[512,512]{0,1:T(8,128)}) %reduce-scatter.2.cloned.1.call-update) | async-done | bytes 1048592 | tf_op jit(solution)/shard_map/reduce_scatter | solution.py:65
  517.0 4.4 scatter_custom_fusion
  521.4 10.2 %all-to-all-start.2 = ((f32[512,32,32]{0,2,1:T(8,128)}), f32[512,32,32]{0,2,1:T(8,128)}, u32[]{:S(2)}, u32[]{:S(2)}) async-start(f32[512,32,32]{0,2,1:T(8,128)} %bitcast.46), calls=%async_computation.3 | async-start | bytes 4194304 | tf_op jit(solution)/shard_map/all_to_all | solution.py:74
  531.6 0.0 all-reduce.2.cloned.1.call-start
  531.6 0.1 broadcast_in_dim.36
  531.7 3.9 fusion.23
  535.6 0.8 broadcast_multiply_fusion
  536.4 0.0 all-reduce.2.cloned.1.call-update
  536.5 0.0 copy-start.4
  536.5 5.0 convolution_convert_fusion.1
  541.4 0.0 copy-done.4
  541.4 0.0 copy-start.1
  541.4 2.6 convolution_convert_fusion
  544.1 34.9 %all-to-all-done.2 = f32[512,32,32]{0,2,1:T(8,128)} async-done(((f32[512,32,32]{0,2,1:T(8,128)}), f32[512,32,32]{0,2,1:T(8,128)}, u32[]{:S(2)}, u32[]{:S(2)}) %all-to-all-start.2) | async-done | bytes 2097184 | tf_op jit(solution)/shard_map/all_to_all | solution.py:74
  579.0 3.2 bitcast_select_fusion
  582.2 7.6 scatter_custom_fusion.1
  589.8 0.7 convert_bitcast_fusion
  590.5 207.0 %all-reduce.2.cloned.1.call-done = f32[4096,16]{0,1:T(8,128)} async-done(((f32[4096,16]{0,1:T(8,128)}), f32[4096,16]{0,1:T(8,128)}) %all-reduce.2.cloned.1.call-update) | async-done | bytes 262160 | tf_op jit(solution)/shard_map/psum | solution.py:63
  797.6 1.7 copy.11
  799.3 0.0 copy-done.1
  (13 shorter events, 0.1 us)
Async XLA Ops:
  8.0 7.3 copy-start
  8.0 1.2 copy-start.2
  244.1 192.7 %all-to-all-start.1 = ((bf16[32,32,4096]{2,1,0:T(8,128)(2,1)}), bf16[32,32,4096]{2,1,0:T(8,128)(2,1)}, u32[]{:S(2)}, u32[]{:S(2)}) async-start(bf16[32,32,4096]{2,1,0:T(8,128)(2,1)} %get-tuple-element.36), calls=%async_computation.1 | async-start | bytes 16777216 | tf_op jit(solution)/shard_map/all_to_all | solution.py:34
  251.8 265.1 %reduce-scatter.2.cloned.1.call-start = ((), (), s32[]{:S(2)}) async-start(), calls=%async_computation.4 | async-start | bytes 9437184 | tf_op jit(solution)/shard_map/reduce_scatter | solution.py:65
  274.5 16.9 %copy-start.5 = (bf16[4096,256]{1,0:T(8,128)(2,1)S(1)}, bf16[4096,256]{1,0:T(8,128)(2,1)}, u32[]{:S(2)}) copy-start(bf16[4096,256]{1,0:T(8,128)(2,1)} %param.8) | copy-start | bytes 6291460
  287.9 3.5 copy-start.3
  521.4 57.6 %all-to-all-start.2 = ((f32[512,32,32]{0,2,1:T(8,128)}), f32[512,32,32]{0,2,1:T(8,128)}, u32[]{:S(2)}, u32[]{:S(2)}) async-start(f32[512,32,32]{0,2,1:T(8,128)} %bitcast.46), calls=%async_computation.3 | async-start | bytes 4194304 | tf_op jit(solution)/shard_map/all_to_all | solution.py:74
  531.6 266.0 %all-reduce.2.cloned.1.call-start = ((), (), s32[]{:S(2)}) async-start(), calls=%async_computation.5 | async-start | bytes 524288 | tf_op jit(solution)/shard_map/psum | solution.py:63
  536.5 5.0 copy-start.4
  541.4 257.8 %copy-start.1 = (bf16[256,4096]{1,0:T(8,128)(2,1)S(1)}, bf16[256,4096]{1,0:T(8,128)(2,1)}, u32[]{:S(2)}) copy-start(bf16[256,4096]{1,0:T(8,128)(2,1)} %param.7) | copy-start | bytes 6291460
Sparse Core Ops, SparseCore 0:
  459.4 57.4 reduce-scatter.1
Sparse Core Ops, SparseCore 1:
  538.1 259.4 all-reduce.1
where the time goes:
time: 808 us; the launch traced here: 807 us
  waiting for transfers between devices  444 us (55%)
  blocking collectives  195 us (24%)
  local copies, waits for them, and re-layouts  65.6 us (8%)
  other arithmetic  43 us (5%)
  matrix products  25.8 us (3%)
  starting transfers between devices  18 us (2%)
  between operations  15.7 us (2%)
    psum x1, waiting for transfers between devices, body(): grad_router = lax.psum(router_term, ('expert', 'tensor'))  207 us
    all_to_all x1, blocking collectives, body(): lax.all_to_all(pack(tokens), 'expert', split_axis=0, concat_axis=0, tiled...  195 us
    all_to_all x1, waiting for transfers between devices, body(): lax.all_to_all(pack(cotangent), 'expert', split_axis=0, concat_axis=0, ti...  144 us
    reduce_scatter x1, waiting for transfers between devices, body(): lax.psum_scatter(jnp.dot(w_in, pre_grad.T, preferred_element_type=jnp.flo...  57.6 us
    all_to_all x1, waiting for transfers between devices, body(): lax.all_to_all(outgoing.reshape(share, n_expert, bucket), 'expert', split...  34.9 us
    gather x2, local copies, waits for them, and re-layouts, pack(): source[send_rows]  24.8 us
    gather x3, other arithmetic, body(): run_start[home_index]  20 us
  transfers between devices with their start and end apart: 4, of which 4 were waited for; matrix products, arithmetic and copies ran while one was open for 8% of the time, Pallas kernels for 0%

commit v1 on v0

--- a/solution.py
+++ b/solution.py
@@ -2,6 +2,12 @@
 import jax.numpy as jnp
 from jax import lax
 from jax.sharding import PartitionSpec as P
+
+
+def add_all(value, axis):
+    parts = lax.all_gather(value, axis, axis=0, tiled=False)
+    result = parts.sum(axis=0)
+    return result
 
 
 def body(tokens, cotangent, w_in, w_out, router, chosen):
@@ -60,7 +66,7 @@
     router_term = (
         router_col[:, None] * (jnp.arange(expert_total) == expert).astype(jnp.float32)[None, :]
     )
-    grad_router = lax.psum(router_term, ("expert", "tensor"))
+    grad_router = add_all(router_term, ("expert", "tensor"))
     router_rows = r_col.astype(jnp.float32)
     summed = lax.psum_scatter(
         jnp.dot(w_in, pre_grad.T, preferred_element_type=jnp.float32)

time: 808 us -> 755 us (0.934)
  waiting for transfers between devices: 444 us -> 372 us
  other arithmetic: 43 us -> 63.3 us
    psum x1 -> x0, waiting for transfers between devices: 207 us -> none  [body(): grad_router = lax.psum(router_term, ('expert', 'tensor'))]
    all_gather x0 -> x1, waiting for transfers between devices: none -> 116 us  [add_all(): parts = lax.all_gather(value, axis, axis=0, tiled=False)]
    reduce_sum x0 -> x1, other arithmetic: none -> 21.8 us  [add_all(): result = parts.sum(axis=0)]
    all_to_all x1, waiting for transfers between devices: 34.9 us -> 56.2 us  [body(): lax.all_to_all(outgoing.reshape(share, n_expert, bucket), 'expert', split...]
  transfers between devices with their start and end apart: 4 -> 4, of which waited for: 4 -> 4; matrix products, arithmetic and copies ran while one was open for 8% -> 9% of each run, Pallas kernels for 0% -> 0%
where the time goes in v1:
time: 755 us; the launch traced here: 753 us
  waiting for transfers between devices  372 us (49%)
  blocking collectives  195 us (26%)
  local copies, waits for them, and re-layouts  64.2 us (9%)
  other arithmetic  63.3 us (8%)
  matrix products  25.7 us (3%)
  starting transfers between devices  17.9 us (2%)
  between operations  15.7 us (2%)
    all_to_all x1, blocking collectives, body(): lax.all_to_all(pack(tokens), 'expert', split_axis=0, concat_axis=0, tiled...  195 us
    all_to_all x1, waiting for transfers between devices, body(): lax.all_to_all(pack(cotangent), 'expert', split_axis=0, concat_axis=0, ti...  144 us
    all_gather x1, waiting for transfers between devices, add_all(): parts = lax.all_gather(value, axis, axis=0, tiled=False)  116 us
    all_to_all x1, waiting for transfers between devices, body(): lax.all_to_all(outgoing.reshape(share, n_expert, bucket), 'expert', split...  56.2 us
    reduce_scatter x1, waiting for transfers between devices, body(): lax.psum_scatter(jnp.dot(w_in, pre_grad.T, preferred_element_type=jnp.flo...  55.6 us
    gather x2, local copies, waits for them, and re-layouts, pack(): source[send_rows]  24.8 us
    reduce_sum x1, other arithmetic, add_all(): result = parts.sum(axis=0)  21.8 us
    gather x3, other arithmetic, body(): run_start[home_index]  20 us
  transfers between devices with their start and end apart: 4, of which 4 were waited for; matrix products, arithmetic and copies ran while one was open for 9% of the time, Pallas kernels for 0%

profile of v1, /device:TPU:2, one launch (start us, length us, event | category | flops | bytes accessed | tf_op | source)
XLA Modules:
  0.0 753.4 jit_solution(3489701042617409861)
XLA Ops:
  8.0 0.0 copy-start
  8.0 0.0 copy-start.2
  8.1 1.0 convert_reduce_fusion.2
  9.1 0.1 fusion.13
  9.2 0.1 reshape.459
  9.2 0.0 copy-done.2
  9.2 4.5 gather_fusion.6
  13.8 0.1 reshape.462
  13.8 0.1 iota_compare_fusion
  13.9 0.1 subtract_select_fusion
  14.0 0.6 gather_fusion
  14.6 0.1 reshape.366
  14.7 0.6 gather_fusion.1
  15.3 0.0 copy-done
  15.3 7.8 %gather_fusion.4 = bf16[1024,4096]{1,0:T(8,128)(2,1)} fusion(bf16[256,4096]{1,0:T(8,128)(2,1)S(1)} %copy-done, s32[1024]{0:T(1024)S(1)} %broadcast_clamp_fusion), kind=kCustom, calls=%fused_computation.4 | custom fusion | bytes 16781312 | tf_op jit(solution)/shard_map/gather | solution.py:35
  23.1 16.9 %gather_fusion.2 = bf16[1024,4096]{1,0:T(8,128)(2,1)} fusion(bf16[256,4096]{1,0:T(8,128)(2,1)} %param.6, s32[1024]{0:T(1024)S(1)} %broadcast_clamp_fusion), kind=kCustom, calls=%fused_computation.2 | custom fusion | bytes 16781312 | tf_op jit(solution)/shard_map/gather | solution.py:35
  40.0 9.2 %broadcast_select_fusion = (bf16[32,32,4096]{2,1,0:T(8,128)(2,1)}, bf16[32,32,4096]{2,1,0:T(8,128)(2,1)S(1)}) fusion(bf16[32,32,4096]{2,1,0:T(8,128)(2,1)} %bitcast.83, pred[32,32]{1,0:T(8,128)(4,1)S(1)} %gather_fusion.1, bf16[32,32,4096]{2,1,0:T(8,128)(2,1)} %bitcast.84), kind=kLoop, calls=%fused_computation.10 | loop fusion | flops 8388608 | bytes 33555456 | tf_op jit(solution)/shard_map/jit(_where)/select_n | solution.py:35
  49.2 194.9 %all_to_all.15 = bf16[32,32,4096]{2,1,0:T(8,128)(2,1)} all-to-all(bf16[32,32,4096]{2,1,0:T(8,128)(2,1)S(1)} %get-tuple-element.37), channel_id=1, replica_groups=mesh['expert'=32,'tensor'=8] {'expert'}, dimensions={0} | all-to-all | bytes 16777216 | tf_op jit(solution)/shard_map/all_to_all | solution.py:39
  244.1 7.7 %all-to-all-start.1 = ((bf16[32,32,4096]{2,1,0:T(8,128)(2,1)}), bf16[32,32,4096]{2,1,0:T(8,128)(2,1)}, u32[]{:S(2)}, u32[]{:S(2)}) async-start(bf16[32,32,4096]{2,1,0:T(8,128)(2,1)} %get-tuple-element.36), calls=%async_computation.1 | async-start | bytes 16777216 | tf_op jit(solution)/shard_map/all_to_all | solution.py:40
  251.8 0.0 reduce-scatter.2.cloned.1.call-start
  251.9 0.9 dynamic-slice_reduce_fusion
  252.8 0.2 convert_reduce_fusion
  253.0 0.7 fusion.21
  253.7 4.3 compare_select_fusion.5
  258.1 0.7 fusion.20
  258.8 0.2 compare_reduce_fusion.24
  258.9 15.5 %select_select_fusion = s32[512]{0:T(512)S(1)} fusion(pred[512]{0:T(512)(128)(4,1)S(1)} %get-tuple-element.30, pred[512]{0:T(512)(128)(4,1)S(1)} %get-tuple-element.29, pred[512]{0:T(512)(128)(4,1)S(1)} %get-tuple-element.28, pred[512]{0:T(512)(128)(4,1)S(1)} %get-tuple-element.27, pred[512]{0:T(512)(128)(4,1)S(1)} %get-tuple-element.26, ...), kind=kLoop, calls=%fused_computation.88 | loop fusion | flops 12800 | bytes 16996 | tf_op jit(solution)/shard_map/gather | solution.py:46
  274.5 0.0 copy-start.5
  274.5 13.4 %gather_fusion.3 = bf16[512,4096]{1,0:T(8,128)(2,1)} fusion(bf16[1024,4096]{1,0:T(8,128)(2,1)} %bitcast.82, s32[1024]{0:T(1024)S(1)} %pad_clamp_fusion), kind=kCustom, calls=%fused_computation.3 | custom fusion | bytes 8390656 | tf_op jit(solution)/shard_map/gather | solution.py:47
  287.9 0.0 copy-start.3
  287.9 3.5 fusion.9
  291.4 0.0 copy-done.5
  291.4 0.0 copy-done.3
  291.5 1.3 fusion.22
  292.8 144.1 %all-to-all-done.1 = bf16[32,32,4096]{2,1,0:T(8,128)(2,1)} async-done(((bf16[32,32,4096]{2,1,0:T(8,128)(2,1)}), bf16[32,32,4096]{2,1,0:T(8,128)(2,1)}, u32[]{:S(2)}, u32[]{:S(2)}) %all-to-all-start.1) | async-done | bytes 8388640 | tf_op jit(solution)/shard_map/all_to_all | solution.py:40
  436.9 13.0 %gather_fusion.5 = bf16[512,4096]{1,0:T(8,128)(2,1)} fusion(bf16[1024,4096]{1,0:T(8,128)(2,1)} %bitcast.43, s32[1024]{0:T(1024)S(1)} %pad_clamp_fusion), kind=kCustom, calls=%fused_computation.5 | custom fusion | bytes 8390656 | tf_op jit(solution)/shard_map/gather | solution.py:48
  449.9 4.3 multiply_reduce_fusion
  454.2 5.1 bitcast_add_fusion
  459.3 0.0 reduce-scatter.2.cloned.1.call-update
  459.3 0.0 all-gather.2.cloned.1.call-start
  459.4 3.9 fusion.23
  463.3 0.8 broadcast_multiply_fusion
  464.1 0.0 all-gather.2.cloned.1.call-update
  464.1 55.6 %reduce-scatter.2.cloned.1.call-done = f32[512,512]{0,1:T(8,128)} async-done(((f32[4096,512]{0,1:T(8,128)}), f32[512,512]{0,1:T(8,128)}) %reduce-scatter.2.cloned.1.call-update) | async-done | bytes 1048592 | tf_op jit(solution)/shard_map/reduce_scatter | solution.py:71
  519.7 4.6 scatter_custom_fusion
  524.3 10.2 %all-to-all-start.2 = ((f32[512,32,32]{0,2,1:T(8,128)}), f32[512,32,32]{0,2,1:T(8,128)S(1)}, u32[]{:S(2)}, u32[]{:S(2)}) async-start(f32[512,32,32]{0,2,1:T(8,128)} %bitcast.85), calls=%async_computation.3 | async-start | bytes 4194304 | tf_op jit(solution)/shard_map/all_to_all | solution.py:80
  534.5 0.1 broadcast_in_dim.36
  534.6 0.0 copy-start.4
  534.6 5.0 convolution_convert_fusion.1
  539.6 0.0 copy-done.4
  539.6 2.6 convolution_convert_fusion
  542.2 56.2 %all-to-all-done.2 = f32[512,32,32]{0,2,1:T(8,128)S(1)} async-done(((f32[512,32,32]{0,2,1:T(8,128)}), f32[512,32,32]{0,2,1:T(8,128)S(1)}, u32[]{:S(2)}, u32[]{:S(2)}) %all-to-all-start.2) | async-done | bytes 2097184 | tf_op jit(solution)/shard_map/all_to_all | solution.py:80
  598.5 1.6 bitcast_select_fusion
  600.0 7.6 %scatter_custom_fusion.1 = f32[512,256]{0,1:T(8,128)S(1)} fusion(s32[1024]{0:T(1024)S(1)} %bitcast.91, f32[512,1024]{0,1:T(8,128)} %bitcast_select_fusion, f32[]{:T(128)} %constant.70.clone.1), kind=kCustom, calls=%fused_computation.14 | custom fusion | flops 524288 | bytes 2621444 | tf_op jit(solution)/shard_map/scatter-add | solution.py:84
  607.6 0.7 convert_bitcast_fusion
  608.4 115.8 %all-gather.2.cloned.1.call-done = f32[256,4096,16]{1,2,0:T(8,128)} async-done(((f32[1,4096,16]{1,2,0:T(8,128)}), f32[256,4096,16]{1,2,0:T(8,128)}) %all-gather.2.cloned.1.call-update) | async-done | bytes 67108880 | tf_op jit(solution)/shard_map/all_gather | solution.py:8
  724.1 0.0 copy-start.1
  724.1 21.8 %reduce_sum.49 = f32[4096,16]{0,1:T(8,128)} reduce(f32[256,4096,16]{1,2,0:T(8,128)} %all-gather.2.cloned.1.call-done, f32[]{:T(128)} %constant.70.clone.1), dimensions={0}, to_apply=%region_7.8 | reduce | flops 16711680 | bytes 67371008 | tf_op jit(solution)/shard_map/reduce_sum | solution.py:9
  746.0 0.0 copy-done.1
  (13 shorter events, 0.1 us)
Async XLA Ops:
  8.0 7.3 copy-start
  8.0 1.2 copy-start.2
  244.1 192.7 %all-to-all-start.1 = ((bf16[32,32,4096]{2,1,0:T(8,128)(2,1)}), bf16[32,32,4096]{2,1,0:T(8,128)(2,1)}, u32[]{:S(2)}, u32[]{:S(2)}) async-start(bf16[32,32,4096]{2,1,0:T(8,128)(2,1)} %get-tuple-element.36), calls=%async_computation.1 | async-start | bytes 16777216 | tf_op jit(solution)/shard_map/all_to_all | solution.py:40
  251.8 267.9 %reduce-scatter.2.cloned.1.call-start = ((), (), s32[]{:S(2)}) async-start(), calls=%async_computation.4 | async-start | bytes 9437184 | tf_op jit(solution)/shard_map/reduce_scatter | solution.py:71
  274.5 16.9 %copy-start.5 = (bf16[4096,256]{1,0:T(8,128)(2,1)S(1)}, bf16[4096,256]{1,0:T(8,128)(2,1)}, u32[]{:S(2)}) copy-start(bf16[4096,256]{1,0:T(8,128)(2,1)} %param.8) | copy-start | bytes 6291460
  287.9 3.5 copy-start.3
  459.3 264.9 %all-gather.2.cloned.1.call-start = ((), (), s32[]{:S(2)}) async-start(), calls=%async_computation.5 | async-start | bytes 67371008 | tf_op jit(solution)/shard_map/all_gather | solution.py:8
  524.3 74.1 %all-to-all-start.2 = ((f32[512,32,32]{0,2,1:T(8,128)}), f32[512,32,32]{0,2,1:T(8,128)S(1)}, u32[]{:S(2)}, u32[]{:S(2)}) async-start(f32[512,32,32]{0,2,1:T(8,128)} %bitcast.85), calls=%async_computation.3 | async-start | bytes 4194304 | tf_op jit(solution)/shard_map/all_to_all | solution.py:80
  534.6 5.0 copy-start.4
  724.1 21.8 %copy-start.1 = (bf16[256,4096]{1,0:T(8,128)(2,1)S(1)}, bf16[256,4096]{1,0:T(8,128)(2,1)}, u32[]{:S(2)}) copy-start(bf16[256,4096]{1,0:T(8,128)(2,1)} %param.7) | copy-start | bytes 6291460
Sparse Core Ops, SparseCore 0:
  459.4 60.2 reduce-scatter.1
Sparse Core Ops, SparseCore 1:
  464.2 259.9 all-gather.1
